TPU v7x, 1024 devices: a whole 4x4x32 slice. The times are simulated.
1024 devices in a mesh: blk: 32 (over z), head: 32 (over x, y, core).
Axes of the slice: x: 4, y: 4, z: 32, core: 2. Of those that a mesh axis runs over, the one named last changes fastest.
Arguments:
- query: bfloat16 [16384, 8192], P(('blk', 'head')), may hold values from -6 to 6
- key: bfloat16 [16384, 1024], P(('blk', 'head')), may hold values from -6 to 6
- value: bfloat16 [16384, 1024], P(('blk', 'head')), may hold values from -6 to 6
- grad_out: bfloat16 [16384, 8192], P(('blk', 'head')), may hold values from -6 to 6
- order: int32 [32, 2], replicated, may hold values from 0 to 63, as said below
Outputs:
- attn_out: bfloat16 [16384, 8192], P('blk', 'head')
- grad_query: bfloat16 [16384, 8192], P(('blk', 'head'))
- grad_key: bfloat16 [16384, 1024], P(('blk', 'head'))
- grad_value: bfloat16 [16384, 1024], P(('blk', 'head'))
Inputs may be any that keep to these rules, and one draw needn't show every extreme that they name: Row r names the two sequence segments held by block position r: some c and 63 - c, in either order; every segment appears exactly once.
All inputs are finite; a program needn't handle non-finite values.
Results may differ from a plain program's by a relative error of at most 0.03.
Values may be sent and summed in bfloat16 or wider, within the bound.
No kernel may reach another device: no remote copies, remote signals or barrier semaphores. Data moves between devices by JAX's collectives and lax.ppermute only.
A program may use at most 32 MiB of HBM per device.

v0:
```python
import math

import jax
import jax.numpy as jnp
from jax import lax
from jax.sharding import PartitionSpec as P

KEY_VALUE_HEADS = 8
HEAD_SIZE = 128
WINDOW_BLOCKS = 3


neg_big = -1e30


def shifted(block, axis, distance):
    devices = range(lax.axis_size(axis))
    route = [((i - distance) % len(devices), i) for i in devices]
    return lax.ppermute(block, axis, route)


def segment_rows(segment_list, half_rows):
    offsets = jnp.arange(half_rows, dtype=jnp.int32)
    return jnp.concatenate(
        [segment_list[0] * half_rows + offsets, segment_list[1] * half_rows + offsets]
    )


def per_device(query, key, value, grad_out, order):
    head_total = lax.axis_size("head")
    n_blk = lax.axis_size("blk")
    nearby_rows = query.shape[0]
    head_copies = head_total // KEY_VALUE_HEADS
    key_expanded = jnp.repeat(
        key.reshape(nearby_rows, KEY_VALUE_HEADS, HEAD_SIZE), head_copies, axis=1
    ).reshape(nearby_rows, head_total * HEAD_SIZE)
    value_expanded = jnp.repeat(
        value.reshape(nearby_rows, KEY_VALUE_HEADS, HEAD_SIZE), head_copies, axis=1
    ).reshape(nearby_rows, head_total * HEAD_SIZE)
    q_heads, k_heads, v_heads, g_heads = (
        lax.all_to_all(query, "head", split_axis=1, concat_axis=0, tiled=True),
        lax.all_to_all(key_expanded, "head", split_axis=1, concat_axis=0, tiled=True),
        lax.all_to_all(value_expanded, "head", split_axis=1, concat_axis=0, tiled=True),
        lax.all_to_all(grad_out, "head", split_axis=1, concat_axis=0, tiled=True),
    )
    window_rows = q_heads.shape[0]
    half_rows = window_rows // 2
    local_heads = q_heads.shape[1] // HEAD_SIZE
    scale = 1.0 / math.sqrt(HEAD_SIZE)
    queries = q_heads.reshape(window_rows, local_heads, HEAD_SIZE)
    grads = g_heads.reshape(window_rows, local_heads, HEAD_SIZE)
    blocks = [jnp.stack([k_heads, v_heads])]
    for lag_index in range(1, WINDOW_BLOCKS):
        blocks.append(shifted(blocks[-1], "blk", 1))
    my_block = lax.axis_index("blk")
    my_segments = lax.dynamic_slice_in_dim(order, my_block, 1, 0)[0]
    query_pos = segment_rows(my_segments, half_rows)
    key_segments = []
    key_pos = []
    for lag_index in range(WINDOW_BLOCKS):
        source = (my_block - lag_index) % n_blk
        found = lax.dynamic_slice_in_dim(order, source, 1, 0)[0]
        key_segments.append(found)
        key_pos.append(segment_rows(found, half_rows))
    tiles = [(0, 0, window_rows)]

    def sweep(visit, carry):
        for lag_index in range(WINDOW_BLOCKS):
            q_start, k_start, width = tiles[0]

            def apply(state, lag_index=lag_index, q_start=q_start, k_start=k_start, width=width):
                return visit(state, lag_index, q_start, k_start, width)

            carry = apply(carry)
        return carry

    def tile_scores(lag_index, k_start, width):
        k_part = blocks[lag_index][0, k_start : k_start + width]
        raw_scores = (
            jnp.einsum("qhd,kd->hqk", queries, k_part, preferred_element_type=jnp.float32) * scale
        )
        allowed = key_pos[lag_index][None, :] <= query_pos[:, None]
        return (raw_scores, allowed)

    def gather_stats(state, lag_index, q_start, k_start, width):
        run_max, run_sum = state
        raw_scores, allowed = tile_scores(lag_index, k_start, width)
        masked = jnp.where(allowed, raw_scores, neg_big)
        new_max = jnp.maximum(run_max, jnp.max(masked, axis=2))
        weights = jnp.where(allowed, jnp.exp(masked - new_max[:, :, None]), 0.0)
        new_sum = run_sum * jnp.exp(run_max - new_max) + jnp.sum(weights, axis=2)
        return (
            run_max.at[:, q_start : q_start + width].set(new_max),
            run_sum.at[:, q_start : q_start + width].set(new_sum),
        )

    start_max = jnp.full((local_heads, window_rows), neg_big, jnp.float32)
    start_sum = jnp.zeros((local_heads, window_rows), jnp.float32)
    run_max, run_sum = sweep(gather_stats, (start_max, start_sum))
    log_total = run_max + jnp.log(run_sum)

    def tile_weights(lag_index, q_start, k_start, width):
        raw_scores, allowed = tile_scores(lag_index, k_start, width)
        return jnp.where(
            allowed, jnp.exp(raw_scores - log_total[:, q_start : q_start + width, None]), 0.0
        )

    def add_output(accum, lag_index, q_start, k_start, width):
        probs_low = tile_weights(lag_index, q_start, k_start, width).astype(jnp.bfloat16)
        v_part = blocks[lag_index][1, k_start : k_start + width]
        term = jnp.einsum("hqk,kd->qhd", probs_low, v_part, preferred_element_type=jnp.float32)
        return accum.at[q_start : q_start + width].add(term)

    attn = sweep(add_output, jnp.zeros((window_rows, local_heads, HEAD_SIZE), jnp.float32)).astype(
        jnp.bfloat16
    )
    delta = jnp.sum(attn.astype(jnp.float32) * grads.astype(jnp.float32), axis=2).T

    def add_grads(state, lag_index, q_start, k_start, width):
        q_acc, k_acc, v_acc = state
        probs = tile_weights(lag_index, q_start, k_start, width)
        probs_low = probs.astype(jnp.bfloat16)
        k_part = blocks[lag_index][0, k_start : k_start + width]
        v_part = blocks[lag_index][1, k_start : k_start + width]
        d_probs = jnp.einsum("qhd,kd->hqk", grads, v_part, preferred_element_type=jnp.float32)
        d_scores = (probs * (d_probs - delta[:, q_start : q_start + width, None])).astype(
            jnp.bfloat16
        )
        q_acc = q_acc.at[q_start : q_start + width].add(
            jnp.einsum("hqk,kd->qhd", d_scores, k_part, preferred_element_type=jnp.float32)
        )
        k_acc = k_acc.at[lag_index, k_start : k_start + width].add(
            jnp.einsum("hqk,qhd->kd", d_scores, queries, preferred_element_type=jnp.float32)
        )
        v_acc = v_acc.at[lag_index, k_start : k_start + width].add(
            jnp.einsum("hqk,qhd->kd", probs_low, grads, preferred_element_type=jnp.float32)
        )
        return (q_acc, k_acc, v_acc)

    start_q = jnp.zeros((window_rows, local_heads, HEAD_SIZE), jnp.float32)
    start_kv = jnp.zeros((WINDOW_BLOCKS, window_rows, HEAD_SIZE), jnp.float32)
    q_acc, k_acc, v_acc = sweep(add_grads, (start_q, start_kv, start_kv))
    partials = [
        jnp.stack([k_acc[lag_index] * scale, v_acc[lag_index]])
        for lag_index in range(WINDOW_BLOCKS)
    ]
    home_sum = partials[WINDOW_BLOCKS - 1]
    for lag_index in range(WINDOW_BLOCKS - 2, -1, -1):
        home_sum = shifted(home_sum, "blk", -1) + partials[lag_index]
    q_grad = (q_acc * scale).reshape(window_rows, local_heads * HEAD_SIZE)
    dq_tokens, key_grad_tokens, value_grad_tokens = (
        lax.all_to_all(
            q_grad.astype(jnp.bfloat16), "head", split_axis=0, concat_axis=1, tiled=True
        ).astype(q_grad.dtype),
        lax.all_to_all(
            home_sum[0].astype(jnp.bfloat16), "head", split_axis=0, concat_axis=1, tiled=True
        ).astype(jnp.float32),
        lax.all_to_all(
            home_sum[1].astype(jnp.bfloat16), "head", split_axis=0, concat_axis=1, tiled=True
        ).astype(jnp.float32),
    )
    grad_query = dq_tokens.astype(jnp.bfloat16)
    grad_key = (
        jnp.sum(
            key_grad_tokens.reshape(nearby_rows, KEY_VALUE_HEADS, head_copies, HEAD_SIZE), axis=2
        )
        .reshape(nearby_rows, KEY_VALUE_HEADS * HEAD_SIZE)
        .astype(jnp.bfloat16)
    )
    grad_value = (
        jnp.sum(
            value_grad_tokens.reshape(nearby_rows, KEY_VALUE_HEADS, head_copies, HEAD_SIZE), axis=2
        )
        .reshape(nearby_rows, KEY_VALUE_HEADS * HEAD_SIZE)
        .astype(jnp.bfloat16)
    )
    return (attn.reshape(window_rows, local_heads * HEAD_SIZE), grad_query, grad_key, grad_value)


def solution(mesh):
    in_specs = (
        P(("blk", "head"), None),
        P(("blk", "head"), None),
        P(("blk", "head"), None),
        P(("blk", "head"), None),
        P(),
    )
    out_specs = (
        P("blk", "head"),
        P(("blk", "head"), None),
        P(("blk", "head"), None),
        P(("blk", "head"), None),
    )
    return jax.shard_map(
        per_device, mesh=mesh, in_specs=in_specs, out_specs=out_specs, check_vma=False
    )
```

profile of v0, /device:TPU:1, one launch (start us, length us, event | category | flops | bytes accessed | tf_op | source)
XLA Modules:
  0.0 157.6 jit_solution(3298786945764333001)
XLA Ops:
  0.6 0.7 copy-done
  1.4 0.7 broadcast_in_dim.80
  2.1 17.6 %all-to-all-start = ((bf16[16,32,128]{2,0,1:T(8,128)(2,1)}), bf16[16,32,128]{2,0,1:T(8,128)(2,1)S(1)}, u32[]{:S(2)}, u32[]{:S(2)}) async-start(bf16[16,32,128]{2,0,1:T(8,128)(2,1)} %bitcast.4), calls=%async_computation | async-start | bytes 262144 | tf_op jit(solution)/shard_map/all_to_all | solution.py:42
  19.8 0.9 constant_dynamic-slice_fusion.3
  20.7 0.6 fusion.53
  22.6 0.6 fusion.51
  25.8 0.8 copy_bitcast_fusion.4
  27.5 0.7 broadcast_in_dim.84
  28.2 7.2 %all-to-all-start.2 = ((bf16[16,32,128]{2,0,1:T(8,128)(2,1)}), bf16[16,32,128]{2,0,1:T(8,128)(2,1)S(1)}, u32[]{:S(2)}, u32[]{:S(2)}) async-start(bf16[16,32,128]{2,0,1:T(8,128)(2,1)} %bitcast.13), calls=%async_computation.2 | async-start | bytes 262144 | tf_op jit(solution)/shard_map/all_to_all | solution.py:43
  36.1 1.7 %copy.216 = bf16[2,32,8,256]{3,2,0,1:T(8,128)(2,1)} copy(bf16[2,32,8,256]{3,2,1,0:T(8,128)(2,1)} %bitcast.258) | data formatting | bytes 524288 | tf_op jit(solution)/shard_map/all_to_all | solution.py:41
  37.8 5.3 %all-to-all-done.2 = bf16[16,32,128]{2,0,1:T(8,128)(2,1)S(1)} async-done(((bf16[16,32,128]{2,0,1:T(8,128)(2,1)}), bf16[16,32,128]{2,0,1:T(8,128)(2,1)S(1)}, u32[]{:S(2)}, u32[]{:S(2)}) %all-to-all-start.2) | async-done | bytes 131104 | tf_op jit(solution)/shard_map/all_to_all | solution.py:43
  43.1 3.9 %all-to-all-start.1 = ((bf16[16,32,256]{2,0,1:T(8,128)(2,1)}), bf16[16,32,256]{2,0,1:T(8,128)(2,1)S(1)}, u32[]{:S(2)}, u32[]{:S(2)}) async-start(bf16[16,32,256]{2,0,1:T(8,128)(2,1)} %bitcast.249), calls=%async_computation.1 | async-start | bytes 524288 | tf_op jit(solution)/shard_map/all_to_all | solution.py:41
  47.0 0.7 copy.215
  47.8 8.3 %all-to-all-done.1 = bf16[16,32,256]{2,0,1:T(8,128)(2,1)S(1)} async-done(((bf16[16,32,256]{2,0,1:T(8,128)(2,1)}), bf16[16,32,256]{2,0,1:T(8,128)(2,1)S(1)}, u32[]{:S(2)}, u32[]{:S(2)}) %all-to-all-start.1) | async-done | bytes 262176 | tf_op jit(solution)/shard_map/all_to_all | solution.py:41
  56.1 3.7 %all-to-all-start.3 = ((bf16[16,32,256]{2,0,1:T(8,128)(2,1)}), bf16[16,32,256]{2,0,1:T(8,128)(2,1)S(1)}, u32[]{:S(2)}, u32[]{:S(2)}) async-start(bf16[16,32,256]{2,0,1:T(8,128)(2,1)} %bitcast.248), calls=%async_computation.3 | async-start | bytes 524288 | tf_op jit(solution)/shard_map/all_to_all | solution.py:44
  60.3 1.9 %collective-permute-start = (bf16[2,512,128]{2,1,0:T(8,128)(2,1)S(1)}, bf16[2,512,128]{2,1,0:T(8,128)(2,1)S(1)}, u32[]{:S(2)}, u32[]{:S(2)}) collective-permute-start(bf16[2,512,128]{2,1,0:T(8,128)(2,1)S(1)} %pad_maximum_fusion.1), channel_id=1, source_target_pairs={{992,0},{0,32},{32,64},{64,96},{96,128},{128,160},{160,192},{192,2... | collective-permute-start | bytes 786440 | tf_op jit(solution)/shard_map/ppermute | solution.py:19
  62.3 6.5 %all-to-all-done.3 = bf16[16,32,256]{2,0,1:T(8,128)(2,1)S(1)} async-done(((bf16[16,32,256]{2,0,1:T(8,128)(2,1)}), bf16[16,32,256]{2,0,1:T(8,128)(2,1)S(1)}, u32[]{:S(2)}, u32[]{:S(2)}) %all-to-all-start.3) | async-done | bytes 262176 | tf_op jit(solution)/shard_map/all_to_all | solution.py:44
  69.7 6.2 %collective-permute-done = bf16[2,512,128]{2,1,0:T(8,128)(2,1)S(1)} collective-permute-done((bf16[2,512,128]{2,1,0:T(8,128)(2,1)S(1)}, bf16[2,512,128]{2,1,0:T(8,128)(2,1)S(1)}, u32[]{:S(2)}, u32[]{:S(2)}) %collective-permute-start) | collective-permute-done | bytes 262176 | tf_op jit(solution)/shard_map/ppermute | solution.py:19
  75.9 1.9 %collective-permute-start.1 = (bf16[2,512,128]{2,1,0:T(8,128)(2,1)S(1)}, bf16[2,512,128]{2,1,0:T(8,128)(2,1)S(1)}, u32[]{:S(2)}, u32[]{:S(2)}) collective-permute-start(bf16[2,512,128]{2,1,0:T(8,128)(2,1)S(1)} %collective-permute-done), channel_id=1, source_target_pairs={{992,0},{0,32},{32,64},{64,96},{96,128},{128,160},{160,192},{192,2... | collective-permute-start | bytes 786440 | tf_op jit(solution)/shard_map/ppermute | solution.py:19
  78.4 7.6 %collective-permute-done.1 = bf16[2,512,128]{2,1,0:T(8,128)(2,1)S(1)} collective-permute-done((bf16[2,512,128]{2,1,0:T(8,128)(2,1)S(1)}, bf16[2,512,128]{2,1,0:T(8,128)(2,1)S(1)}, u32[]{:S(2)}, u32[]{:S(2)}) %collective-permute-start.1) | collective-permute-done | bytes 262176 | tf_op jit(solution)/shard_map/ppermute | solution.py:19
  86.5 0.6 select_reduce_fusion.2
  87.1 0.6 select_reduce_fusion.1
  87.7 0.6 select_reduce_fusion
  88.8 0.6 convolution_bitcast_fusion.5
  89.4 0.7 fusion.22
  90.1 1.4 multiply_reduce_fusion
  91.5 0.8 fusion.5
  92.4 0.8 fusion.1
  93.7 2.1 %collective-permute-start.2 = (f32[2,512,128]{2,1,0:T(8,128)S(1)}, f32[2,512,128]{2,1,0:T(8,128)S(1)}, u32[]{:S(2)}, u32[]{:S(2)}) collective-permute-start(f32[2,512,128]{2,1,0:T(8,128)S(1)} %pad_maximum_fusion), channel_id=1, source_target_pairs={{32,0},{64,32},{96,64},{128,96},{160,128},{192,160},{224,192},{256... | collective-permute-start | bytes 1572872 | tf_op jit(solution)/shard_map/ppermute | solution.py:19
  96.3 0.8 fusion.3
  98.7 8.6 %collective-permute-done.2 = f32[2,512,128]{2,1,0:T(8,128)S(1)} collective-permute-done((f32[2,512,128]{2,1,0:T(8,128)S(1)}, f32[2,512,128]{2,1,0:T(8,128)S(1)}, u32[]{:S(2)}, u32[]{:S(2)}) %collective-permute-start.2) | collective-permute-done | bytes 524320 | tf_op jit(solution)/shard_map/ppermute | solution.py:19
  107.3 0.9 maximum_add_fusion
  108.1 3.3 %collective-permute-start.3 = (f32[2,512,128]{2,1,0:T(8,128)}, f32[2,512,128]{2,1,0:T(8,128)}, u32[]{:S(2)}, u32[]{:S(2)}) collective-permute-start(f32[2,512,128]{2,1,0:T(8,128)} %maximum_add_fusion), channel_id=1, source_target_pairs={{32,0},{64,32},{96,64},{128,96},{160,128},{192,160},{224,192},{256... | collective-permute-start | bytes 1572872 | tf_op jit(solution)/shard_map/ppermute | solution.py:19
  112.0 1.0 copy.155
  113.0 1.8 %convert_element_type.96 = bf16[32,16,256]{2,1,0:T(8,128)(2,1)} reshape(bf16[512,2,128]{2,1,0:T(2,128)(2,1)} %copy.155) | data formatting | bytes 524288 | tf_op jit(solution)/shard_map/convert_element_type | solution.py:153
  114.8 9.9 %all-to-all-start.4 = ((bf16[32,16,256]{2,1,0:T(8,128)(2,1)}), bf16[32,16,256]{2,1,0:T(8,128)(2,1)}, u32[]{:S(2)}, u32[]{:S(2)}) async-start(bf16[32,16,256]{2,1,0:T(8,128)(2,1)} %convert_element_type.96), calls=%async_computation.4 | async-start | bytes 524288 | tf_op jit(solution)/shard_map/all_to_all | solution.py:152
  125.2 1.6 %convolution_bitcast_fusion.6 = f32[1,512,128]{2,1,0:T(8,128)S(1)} fusion(bf16[512,2,128]{0,2,1:T(8,128)(2,1)} %copy-done.5, f32[512,512,2]{1,0,2:T(8,128)S(1)} %copy-done.2, f32[2,512]{1,0:T(2,128)S(1)} %log_add_fusion, pred[512,512]{0,1:T(8,128)(4,1)} %copy-done.3), kind=kOutput, calls=%fused_computation.43 | convolution fusion | flops 136314880 | bytes 2887680 | tf_op jit(solution)/shard_map/hqk,qhd->kd/dot_general | solution.py:136
  126.9 1.1 fusion.31
  128.0 0.7 fusion.50
  128.7 5.1 %all-to-all-done.4 = bf16[32,16,256]{2,1,0:T(8,128)(2,1)} async-done(((bf16[32,16,256]{2,1,0:T(8,128)(2,1)}), bf16[32,16,256]{2,1,0:T(8,128)(2,1)}, u32[]{:S(2)}, u32[]{:S(2)}) %all-to-all-start.4) | async-done | bytes 262176 | tf_op jit(solution)/shard_map/all_to_all | solution.py:152
  133.8 3.7 %all-to-all-start.6 = ((bf16[32,16,128]{2,1,0:T(8,128)(2,1)}), bf16[32,16,128]{2,1,0:T(8,128)(2,1)S(1)}, u32[]{:S(2)}, u32[]{:S(2)}) async-start(bf16[32,16,128]{2,1,0:T(8,128)(2,1)} %bitcast.66), calls=%async_computation.6 | async-start | bytes 262144 | tf_op jit(solution)/shard_map/all_to_all | solution.py:158
  137.5 0.8 copy.165
  138.3 1.7 %copy.188 = bf16[32,2,8,256]{3,2,0,1:T(8,128)(2,1)} copy(bf16[32,2,8,256]{3,2,1,0:T(8,128)(2,1)} %bitcast.86) | data formatting | bytes 524288 | tf_op jit(solution)/shard_map/all_to_all | solution.py:152
  140.0 5.3 %all-to-all-done.6 = bf16[32,16,128]{2,1,0:T(8,128)(2,1)S(1)} async-done(((bf16[32,16,128]{2,1,0:T(8,128)(2,1)}), bf16[32,16,128]{2,1,0:T(8,128)(2,1)S(1)}, u32[]{:S(2)}, u32[]{:S(2)}) %all-to-all-start.6) | async-done | bytes 131104 | tf_op jit(solution)/shard_map/all_to_all | solution.py:158
  145.3 3.9 %all-to-all-start.5 = ((bf16[32,16,128]{2,1,0:T(8,128)(2,1)}), bf16[32,16,128]{2,1,0:T(8,128)(2,1)S(1)}, u32[]{:S(2)}, u32[]{:S(2)}) async-start(bf16[32,16,128]{2,1,0:T(8,128)(2,1)} %bitcast.63), calls=%async_computation.5 | async-start | bytes 262144 | tf_op jit(solution)/shard_map/all_to_all | solution.py:155
  149.2 0.6 copy_bitcast_fusion.2
  149.8 7.1 %all-to-all-done.5 = bf16[32,16,128]{2,1,0:T(8,128)(2,1)S(1)} async-done(((bf16[32,16,128]{2,1,0:T(8,128)(2,1)}), bf16[32,16,128]{2,1,0:T(8,128)(2,1)S(1)}, u32[]{:S(2)}, u32[]{:S(2)}) %all-to-all-start.5) | async-done | bytes 131104 | tf_op jit(solution)/shard_map/all_to_all | solution.py:155
  157.0 0.6 copy_bitcast_fusion.3
  (49 shorter events, 7.0 us)
Async XLA Ops:
  0.6 0.8 copy-start
  1.4 45.6 %copy-start.4 = (bf16[16,8192]{1,0:T(8,128)(2,1)S(1)}, bf16[16,8192]{1,0:T(8,128)(2,1)}, u32[]{:S(2)}) copy-start(bf16[16,8192]{1,0:T(8,128)(2,1)} %param.68) | copy-start | bytes 786436
  2.1 25.4 %all-to-all-start = ((bf16[16,32,128]{2,0,1:T(8,128)(2,1)}), bf16[16,32,128]{2,0,1:T(8,128)(2,1)S(1)}, u32[]{:S(2)}, u32[]{:S(2)}) async-start(bf16[16,32,128]{2,0,1:T(8,128)(2,1)} %bitcast.4), calls=%async_computation | async-start | bytes 262144 | tf_op jit(solution)/shard_map/all_to_all | solution.py:42
  28.2 14.9 %all-to-all-start.2 = ((bf16[16,32,128]{2,0,1:T(8,128)(2,1)}), bf16[16,32,128]{2,0,1:T(8,128)(2,1)S(1)}, u32[]{:S(2)}, u32[]{:S(2)}) async-start(bf16[16,32,128]{2,0,1:T(8,128)(2,1)} %bitcast.13), calls=%async_computation.2 | async-start | bytes 262144 | tf_op jit(solution)/shard_map/all_to_all | solution.py:43
  43.1 13.0 %all-to-all-start.1 = ((bf16[16,32,256]{2,0,1:T(8,128)(2,1)}), bf16[16,32,256]{2,0,1:T(8,128)(2,1)S(1)}, u32[]{:S(2)}, u32[]{:S(2)}) async-start(bf16[16,32,256]{2,0,1:T(8,128)(2,1)} %bitcast.249), calls=%async_computation.1 | async-start | bytes 524288 | tf_op jit(solution)/shard_map/all_to_all | solution.py:41
  56.1 12.8 %all-to-all-start.3 = ((bf16[16,32,256]{2,0,1:T(8,128)(2,1)}), bf16[16,32,256]{2,0,1:T(8,128)(2,1)S(1)}, u32[]{:S(2)}, u32[]{:S(2)}) async-start(bf16[16,32,256]{2,0,1:T(8,128)(2,1)} %bitcast.248), calls=%async_computation.3 | async-start | bytes 524288 | tf_op jit(solution)/shard_map/all_to_all | solution.py:44
  60.3 31.2 %copy-start.3 = (pred[512,512]{0,1:T(8,128)(4,1)}, pred[512,512]{0,1:T(8,128)(4,1)S(1)}, u32[]{:S(2)}) copy-start(pred[512,512]{0,1:T(8,128)(4,1)S(1)} %get-tuple-element.341) | copy-start | bytes 786436
  60.3 15.6 %collective-permute-start = (bf16[2,512,128]{2,1,0:T(8,128)(2,1)S(1)}, bf16[2,512,128]{2,1,0:T(8,128)(2,1)S(1)}, u32[]{:S(2)}, u32[]{:S(2)}) collective-permute-start(bf16[2,512,128]{2,1,0:T(8,128)(2,1)S(1)} %pad_maximum_fusion.1), channel_id=1, source_target_pairs={{992,0},{0,32},{32,64},{64,96},{96,128},{128,160},{160,192},{192,2... | collective-permute-start | bytes 786440 | tf_op jit(solution)/shard_map/ppermute | solution.py:19
  69.1 29.0 %copy-start.5 = (bf16[512,2,128]{0,2,1:T(8,128)(2,1)}, bf16[512,2,128]{0,2,1:T(8,128)(2,1)S(1)}, u32[]{:S(2)}) copy-start(bf16[512,2,128]{0,2,1:T(8,128)(2,1)S(1)} %copy.145) | copy-start | bytes 786436
  69.7 21.9 %copy-start.1 = (f32[512,512,2]{1,0,2:T(8,128)}, f32[512,512,2]{1,0,2:T(8,128)S(1)}, u32[]{:S(2)}) copy-start(f32[512,512,2]{1,0,2:T(8,128)S(1)} %get-tuple-element.361) | copy-start | bytes 6291460
  75.9 10.0 %collective-permute-start.1 = (bf16[2,512,128]{2,1,0:T(8,128)(2,1)S(1)}, bf16[2,512,128]{2,1,0:T(8,128)(2,1)S(1)}, u32[]{:S(2)}, u32[]{:S(2)}) collective-permute-start(bf16[2,512,128]{2,1,0:T(8,128)(2,1)S(1)} %collective-permute-done), channel_id=1, source_target_pairs={{992,0},{0,32},{32,64},{64,96},{96,128},{128,160},{160,192},{192,2... | collective-permute-start | bytes 786440 | tf_op jit(solution)/shard_map/ppermute | solution.py:19
  93.7 13.6 %collective-permute-start.2 = (f32[2,512,128]{2,1,0:T(8,128)S(1)}, f32[2,512,128]{2,1,0:T(8,128)S(1)}, u32[]{:S(2)}, u32[]{:S(2)}) collective-permute-start(f32[2,512,128]{2,1,0:T(8,128)S(1)} %pad_maximum_fusion), channel_id=1, source_target_pairs={{32,0},{64,32},{96,64},{128,96},{160,128},{192,160},{224,192},{256... | collective-permute-start | bytes 1572872 | tf_op jit(solution)/shard_map/ppermute | solution.py:19
  108.1 17.1 %copy-start.2 = (f32[512,512,2]{1,0,2:T(8,128)S(1)}, f32[512,512,2]{1,0,2:T(8,128)}, u32[]{:S(2)}) copy-start(f32[512,512,2]{1,0,2:T(8,128)} %copy-done.1) | copy-start | bytes 6291460
  108.1 18.7 %collective-permute-start.3 = (f32[2,512,128]{2,1,0:T(8,128)}, f32[2,512,128]{2,1,0:T(8,128)}, u32[]{:S(2)}, u32[]{:S(2)}) collective-permute-start(f32[2,512,128]{2,1,0:T(8,128)} %maximum_add_fusion), channel_id=1, source_target_pairs={{32,0},{64,32},{96,64},{128,96},{160,128},{192,160},{224,192},{256... | collective-permute-start | bytes 1572872 | tf_op jit(solution)/shard_map/ppermute | solution.py:19
  114.8 19.0 %all-to-all-start.4 = ((bf16[32,16,256]{2,1,0:T(8,128)(2,1)}), bf16[32,16,256]{2,1,0:T(8,128)(2,1)}, u32[]{:S(2)}, u32[]{:S(2)}) async-start(bf16[32,16,256]{2,1,0:T(8,128)(2,1)} %convert_element_type.96), calls=%async_computation.4 | async-start | bytes 524288 | tf_op jit(solution)/shard_map/all_to_all | solution.py:152
  125.2 12.3 %copy-start.6 = (bf16[512,2,128]{0,2,1:T(8,128)(2,1)S(1)}, bf16[512,2,128]{0,2,1:T(8,128)(2,1)}, u32[]{:S(2)}) copy-start(bf16[512,2,128]{0,2,1:T(8,128)(2,1)} %get-tuple-element.363) | copy-start | bytes 786436
  133.8 11.5 %all-to-all-start.6 = ((bf16[32,16,128]{2,1,0:T(8,128)(2,1)}), bf16[32,16,128]{2,1,0:T(8,128)(2,1)S(1)}, u32[]{:S(2)}, u32[]{:S(2)}) async-start(bf16[32,16,128]{2,1,0:T(8,128)(2,1)} %bitcast.66), calls=%async_computation.6 | async-start | bytes 262144 | tf_op jit(solution)/shard_map/all_to_all | solution.py:158
  145.3 11.7 %all-to-all-start.5 = ((bf16[32,16,128]{2,1,0:T(8,128)(2,1)}), bf16[32,16,128]{2,1,0:T(8,128)(2,1)S(1)}, u32[]{:S(2)}, u32[]{:S(2)}) async-start(bf16[32,16,128]{2,1,0:T(8,128)(2,1)} %bitcast.63), calls=%async_computation.5 | async-start | bytes 262144 | tf_op jit(solution)/shard_map/all_to_all | solution.py:155
where the time goes:
time: 159 us; the launch traced here: 158 us
  waiting for transfers between devices  60.3 us (38%)
  starting transfers between devices  59.2 us (37%)
  local copies, waits for them, and re-layouts  14.9 us (9%)
  matrix products  12.4 us (8%)
  between operations  6.3 us (4%)
  other arithmetic  4.4 us (3%)
    ppermute x4, waiting for transfers between devices, shifted(): return lax.ppermute(block, axis, route)  22.4 us
    all_to_all x1, starting transfers between devices, per_device(): lax.all_to_all(key_expanded, 'head', split_axis=1, concat_axis=0, tiled=T...  17.6 us
    all_to_all x1, starting transfers between devices, per_device(): lax.all_to_all(q_grad.astype(jnp.bfloat16), 'head', split_axis=0, concat_...  9.94 us
    ppermute x4, starting transfers between devices, shifted(): return lax.ppermute(block, axis, route)  9.25 us
    all_to_all x1, waiting for transfers between devices, per_device(): lax.all_to_all(query, 'head', split_axis=1, concat_axis=0, tiled=True)  8.31 us
    all_to_all x1, starting transfers between devices, per_device(): lax.all_to_all(value_expanded, 'head', split_axis=1, concat_axis=0, tiled...  7.2 us
    all_to_all x1, waiting for transfers between devices, per_device(): lax.all_to_all(home_sum[0].astype(jnp.bfloat16), 'head', split_axis=0, co...  7.14 us
    all_to_all x1, waiting for transfers between devices, per_device(): lax.all_to_all(grad_out, 'head', split_axis=1, concat_axis=0, tiled=True)  6.51 us
  transfers between devices with their start and end apart: 11, of which 10 were waited for; matrix products, arithmetic and copies ran while one was open for 13% of the time, Pallas kernels for 0%

commit v1 on v0

v1 whole, which is shorter than its diff:
```python
import math

import jax
import jax.numpy as jnp
from jax import lax
from jax.experimental import pallas as pl
from jax.experimental.pallas import tpu as pltpu
from jax.sharding import PartitionSpec as P


KEY_VALUE_HEADS = 8
HEAD_SIZE = 128
COPIES = 4
HALF = 256
NEG_BIG = -1e30
SCALE = 1.0 / math.sqrt(HEAD_SIZE)
SCALE_LOG2 = SCALE * math.log2(math.e)

F32 = jnp.float32
BF16 = jnp.bfloat16

VMEM = pl.BlockSpec(memory_space=pltpu.VMEM)
SMEM = pl.BlockSpec(memory_space=pltpu.SMEM)


PARAMS = pltpu.CompilerParams(vmem_limit_bytes=16 * 1024 * 1024)


def head_cols(head):
    return slice(head * HEAD_SIZE, (head + 1) * HEAD_SIZE)


def exchange(blocks):
    return lax.all_to_all(blocks, "head", split_axis=0, concat_axis=0, tiled=True)


def shifted(rows, distance):
    count = lax.axis_size("blk")
    route = [((i - distance) % count, i) for i in range(count)]
    return lax.ppermute(rows, "blk", route)


def pack_first(q_hbm, g_hbm, k_hbm, v_hbm, out_ref, kv_ref, q_ref, g_ref, sems):
    moves = [
        pltpu.make_async_copy(k_hbm, kv_ref.at[:, 0:1024], sems.at[0]),
        pltpu.make_async_copy(v_hbm, kv_ref.at[:, 1024:2048], sems.at[1]),
        pltpu.make_async_copy(q_hbm, q_ref, sems.at[2]),
        pltpu.make_async_copy(g_hbm, g_ref, sems.at[3]),
    ]
    for move in moves:
        move.start()
    for part, source in enumerate((kv_ref, q_ref, g_ref)):
        if part == 0:
            moves[0].wait()
            moves[1].wait()
        else:
            moves[part + 1].wait()
        for peer in range(out_ref.shape[0]):
            if part == 0:
                group = peer // COPIES
                out_ref[peer, :, 512:640] = source[:, head_cols(group)]
                out_ref[peer, :, 640:768] = source[:, head_cols(group + KEY_VALUE_HEADS)]
            else:
                at = (part - 1) * 256
                cols = slice(2 * peer * HEAD_SIZE, 2 * (peer + 1) * HEAD_SIZE)
                out_ref[peer, :, at : at + 256] = source[:, cols]


def pack_lags(kv1_ref, kv2_ref, out_ref):
    for peer in range(out_ref.shape[0]):
        group = peer // COPIES
        for lag, kv_ref in enumerate((kv1_ref, kv2_ref)):
            at = lag * 256
            out_ref[peer, :, at : at + 128] = kv_ref[:, head_cols(group)]
            out_ref[peer, :, at + 128 : at + 256] = kv_ref[:, head_cols(group + KEY_VALUE_HEADS)]


def sum_copies(in_ref, group, cols):
    total = in_ref[group * COPIES, :, cols].astype(F32)
    for copy in range(1, COPIES):
        total = total + in_ref[group * COPIES + copy, :, cols].astype(F32)
    return total


def unpack_lags(in_ref, one_ref, two_ref):
    for group in range(KEY_VALUE_HEADS):
        for lag, out_ref in enumerate((one_ref, two_ref)):
            for part in range(2):
                at = lag * 256 + part * 128
                total = sum_copies(in_ref, group, slice(at, at + 128))
                out_ref[:, head_cols(group + part * KEY_VALUE_HEADS)] = total.astype(BF16)


def unpack_last(in_ref, one_ref, two_ref, gq_ref, gk_ref, gv_ref):
    for peer in range(in_ref.shape[0]):
        gq_ref[:, 2 * peer * HEAD_SIZE : 2 * (peer + 1) * HEAD_SIZE] = in_ref[peer, :, 0:256]
    for group in range(KEY_VALUE_HEADS):
        for part, out_ref in enumerate((gk_ref, gv_ref)):
            at = 256 + part * 128
            total = sum_copies(in_ref, group, slice(at, at + 128))
            cols = head_cols(group + part * KEY_VALUE_HEADS)
            total = total + one_ref[:, cols].astype(F32) + two_ref[:, cols].astype(F32)
            out_ref[:, head_cols(group)] = total.astype(BF16)


def dot(a, b):
    return lax.dot_general(a, b, (((1,), (0,)), ((), ())), preferred_element_type=F32)


def dot_nt(a, b):
    return lax.dot_general(a, b, (((1,), (1,)), ((), ())), preferred_element_type=F32)


def attention(order_ref, blk_ref, own_ref, lag_ref, attn_ref, dlag_ref, down_ref, score_ref):
    count = order_ref.shape[0] // 2
    blk = blk_ref[0]

    def low_of(block):
        first, second = order_ref[2 * block], order_ref[2 * block + 1]
        low_first = first < second
        return jnp.where(low_first, 0, HALF), jnp.where(low_first, first, second)

    low, chunk = low_of(blk)
    low1, chunk1 = low_of(lax.rem(blk + (count - 1), count))
    low2, chunk2 = low_of(lax.rem(blk + (count - 2), count))
    below1, below2 = chunk > chunk1, chunk > chunk2

    def at(offset):
        return pl.ds(pl.multiple_of(offset, HALF), HALF)

    lo, hi = at(low), at(HALF - low)
    lo1, hi1 = at(low1), at(HALF - low1)
    lo2, hi2 = at(low2), at(HALF - low2)
    q_dyn1, k_dyn1 = at(jnp.where(below1, low, HALF - low)), at(jnp.where(below1, low1, HALF - low1))
    q_dyn2, k_dyn2 = at(jnp.where(below2, low, HALF - low)), at(jnp.where(below2, low2, HALF - low2))

    tiles = (
        (lo, own_ref, lo, 512, "lo"),
        (hi, own_ref, hi, 512, "hi"),
        (hi, own_ref, lo, 512, "hi"),
        (hi, lag_ref, lo1, 0, "hi"),
        (hi, lag_ref, lo2, 256, "hi"),
        (q_dyn1, lag_ref, k_dyn1, 0, below1),
        (q_dyn2, lag_ref, k_dyn2, 256, below2),
    )
    diagonal = (0, 1)
    causal = lax.broadcasted_iota(jnp.int32, (HALF, HALF), 0) <= lax.broadcasted_iota(
        jnp.int32, (HALF, HALF), 1
    )

    def fold(side, new, low_value, high_value, op):
        if isinstance(side, str):
            if side == "lo":
                return op(low_value, new), high_value
            return low_value, (new if high_value is None else op(high_value, new))
        return (
            jnp.where(side, op(low_value, new), low_value),
            jnp.where(side, high_value, op(high_value, new)),
        )

    def pick(side, low_value, high_value):
        if isinstance(side, str):
            return low_value if side == "lo" else high_value
        return jnp.where(side, low_value, high_value)

    def first_or(op):
        return lambda old, new: new if old is None else op(old, new)

    add = first_or(jnp.add)
    larger = first_or(jnp.maximum)

    d_keys = [None] * len(tiles)
    d_values = [None] * len(tiles)
    keys_t, values_t = [], []
    for _, kv_ref, k_rows, col, _ in tiles:
        keys_t.append(kv_ref[k_rows, col : col + 128].T)
        values_t.append(kv_ref[k_rows, col + 128 : col + 256].T)

    for head in range(2):
        q_cols = head_cols(head)
        g_cols = slice(256 + head * HEAD_SIZE, 256 + (head + 1) * HEAD_SIZE)
        max_lo = max_hi = None
        for index, (q_rows, kv_ref, k_rows, col, side) in enumerate(tiles):
            score = dot_nt(kv_ref[k_rows, col : col + 128], own_ref[q_rows, q_cols]) * SCALE_LOG2
            if index in diagonal:
                score = jnp.where(causal, score, NEG_BIG)
            score_ref[index] = score
            max_lo, max_hi = fold(side, jnp.max(score, axis=0, keepdims=True), max_lo, max_hi, larger)
        sum_lo = sum_hi = None
        for index, (_, _, _, _, side) in enumerate(tiles):
            weights = jnp.exp2(score_ref[index] - pick(side, max_lo, max_hi))
            score_ref[index] = weights
            sum_lo, sum_hi = fold(side, jnp.sum(weights, axis=0, keepdims=True), sum_lo, sum_hi, add)
        inv_lo, inv_hi = 1.0 / sum_lo, 1.0 / sum_hi
        out_lo = out_hi = None
        for index, (_, _, _, _, side) in enumerate(tiles):
            probs = score_ref[index] * pick(side, inv_lo, inv_hi)
            score_ref[index] = probs
            part = dot(values_t[index], probs.astype(BF16))
            out_lo, out_hi = fold(side, part, out_lo, out_hi, add)
        attn_lo, attn_hi = out_lo.T.astype(BF16), out_hi.T.astype(BF16)
        attn_ref[lo, q_cols] = attn_lo
        attn_ref[hi, q_cols] = attn_hi
        delta_lo = jnp.sum(
            (attn_lo.astype(F32) * own_ref[lo, g_cols].astype(F32)).T, axis=0, keepdims=True
        )
        delta_hi = jnp.sum(
            (attn_hi.astype(F32) * own_ref[hi, g_cols].astype(F32)).T, axis=0, keepdims=True
        )
        dq_lo = dq_hi = None
        for index, (q_rows, kv_ref, k_rows, col, side) in enumerate(tiles):
            probs = score_ref[index]
            grads = own_ref[q_rows, g_cols]
            d_probs = dot_nt(kv_ref[k_rows, col + 128 : col + 256], grads)
            d_scores = (probs * (d_probs - pick(side, delta_lo, delta_hi))).astype(BF16)
            d_values[index] = add(d_values[index], dot(probs.astype(BF16), grads))
            d_keys[index] = add(d_keys[index], dot(d_scores, own_ref[q_rows, q_cols]))
            part = dot(keys_t[index], d_scores)
            dq_lo, dq_hi = fold(side, part, dq_lo, dq_hi, add)
        down_ref[lo, q_cols] = (dq_lo * SCALE).T.astype(BF16)
        down_ref[hi, q_cols] = (dq_hi * SCALE).T.astype(BF16)

    for part, scale, found in ((0, SCALE, d_keys), (1, 1.0, d_values)):
        cols = slice(256 + part * 128, 256 + (part + 1) * 128)
        down_ref[hi, cols] = (found[1] * scale).astype(BF16)
        down_ref[lo, cols] = ((found[0] + found[2]) * scale).astype(BF16)
        for lag, (below, lo_k, hi_k) in enumerate(((below1, lo1, hi1), (below2, lo2, hi2))):
            cols = slice(lag * 256 + part * 128, lag * 256 + (part + 1) * 128)
            always, extra = found[3 + lag], found[5 + lag]
            dlag_ref[lo_k, cols] = (jnp.where(below, always + extra, always) * scale).astype(BF16)
            dlag_ref[hi_k, cols] = (jnp.where(below, 0.0, extra) * scale).astype(BF16)


def per_device(query, key, value, grad_out, order):
    peers = lax.axis_size("head")
    rows = query.shape[0]
    window = peers * rows
    shape = jax.ShapeDtypeStruct

    first, kv = pl.pallas_call(
        pack_first,
        out_shape=(shape((peers, rows, 768), BF16), shape((rows, 2048), BF16)),
        in_specs=[pl.BlockSpec(memory_space=pltpu.HBM)] * 4,
        out_specs=(VMEM, VMEM),
        scratch_shapes=[
            pltpu.VMEM((rows, 8192), BF16),
            pltpu.VMEM((rows, 8192), BF16),
            pltpu.SemaphoreType.DMA((4,)),
        ],
        name="pack_first",
    )(query, grad_out, key, value)
    own = exchange(first).reshape(window, 768)
    kv1, kv2 = shifted(kv, 1), shifted(kv, 2)
    lags = pl.pallas_call(
        pack_lags,
        out_shape=shape((peers, rows, 512), BF16),
        in_specs=[VMEM] * 2,
        out_specs=VMEM,
        compiler_params=PARAMS,
        name="pack_lags",
    )(kv1, kv2)
    lag = exchange(lags).reshape(window, 512)

    blk = lax.axis_index("blk").astype(jnp.int32).reshape(1)
    attn, d_lag, d_own = pl.pallas_call(
        attention,
        out_shape=(
            shape((window, 256), BF16),
            shape((window, 512), BF16),
            shape((window, 512), BF16),
        ),
        in_specs=[SMEM, SMEM, VMEM, VMEM],
        out_specs=(VMEM, VMEM, VMEM),
        scratch_shapes=[pltpu.VMEM((7, HALF, HALF), F32)],
        compiler_params=PARAMS,
        name="attention",
    )(order.reshape(-1), blk, own, lag)

    one, two = pl.pallas_call(
        unpack_lags,
        out_shape=(shape((rows, 2048), BF16),) * 2,
        in_specs=[VMEM],
        out_specs=(VMEM, VMEM),
        compiler_params=PARAMS,
        name="unpack_lags",
    )(exchange(d_lag.reshape(peers, rows, 512)))
    one, two = shifted(one, -1), shifted(two, -2)
    grad_query, grad_key, grad_value = pl.pallas_call(
        unpack_last,
        out_shape=(
            shape((rows, 8192), BF16),
            shape((rows, 1024), BF16),
            shape((rows, 1024), BF16),
        ),
        in_specs=[VMEM] * 3,
        out_specs=(VMEM,) * 3,
        compiler_params=PARAMS,
        name="unpack_last",
    )(exchange(d_own.reshape(peers, rows, 512)), one, two)
    return attn, grad_query, grad_key, grad_value


def solution(mesh):
    tokens = P(("blk", "head"), None)
    return jax.shard_map(
        per_device,
        mesh=mesh,
        in_specs=(tokens, tokens, tokens, tokens, P()),
        out_specs=(P("blk", "head"), tokens, tokens, tokens),
        check_vma=False,
    )
```

time: 159 us -> 102 us (0.64)
  starting transfers between devices: 59.2 us -> 24.3 us
  blocking collectives: 0 us -> 34.6 us
  waiting for transfers between devices: 60.3 us -> 32.1 us
  local copies, waits for them, and re-layouts: 14.9 us -> 0.86 us
  matrix products: 12.4 us -> 0 us
  Pallas kernels: 0 us -> 9.16 us
  between operations: 6.3 us -> 0.72 us
  other arithmetic: 4.4 us -> 0 us
    all_to_all x7 -> x2, starting transfers between devices: 50 us -> 7.37 us  [exchange(): lax.all_to_all(blocks, 'head', split_axis=0, concat_axis=0, tiled=True)]
    all_to_all x0 -> x2, blocking collectives: none -> 34.6 us  [exchange(): lax.all_to_all(blocks, 'head', split_axis=0, concat_axis=0, tiled=True)]
    all_to_all x7 -> x2, waiting for transfers between devices: 38 us -> 17 us  [exchange(): lax.all_to_all(blocks, 'head', split_axis=0, concat_axis=0, tiled=True)]
    dot_general x18 -> x0, matrix products: 12.4 us -> none  [the longest x3 2.69 us: add_output(): jnp.einsum('hqk,kd->qhd', probs_low, v_part, preferred_element_type=jnp.f...]
    pallas_call x0 -> x5, Pallas kernels: none -> 9.16 us  [the longest x1 6.25 us: per_device(): pl.pallas_call(attention, out_shape=(shape((window, 256), BF16), shape((w...]
    ppermute x4, starting transfers between devices: 9.25 us -> 16.9 us  [shifted(): return lax.ppermute(rows, 'blk', route)]
    ppermute x4, waiting for transfers between devices: 22.4 us -> 15.1 us  [shifted(): return lax.ppermute(rows, 'blk', route)]
    all_to_all x3 -> x0, local copies, waits for them, and re-layouts: 4.06 us -> none  [the longest x1 1.67 us: per_device(): lax.all_to_all(query, 'head', split_axis=1, concat_axis=0, tiled=True)]
  transfers between devices with their start and end apart: 11 -> 6, of which waited for: 10 -> 4; matrix products, arithmetic and copies ran while one was open for 13% -> 0% of each run, Pallas kernels for 0% -> 0%
where the time goes in v1:
time: 102 us
  blocking collectives  34.6 us (34%)
  waiting for transfers between devices  32.1 us (31%)
  starting transfers between devices  24.3 us (24%)
  Pallas kernels  9.16 us (9%)
    all_to_all x2, blocking collectives, exchange(): lax.all_to_all(blocks, 'head', split_axis=0, concat_axis=0, tiled=True)  34.6 us
    all_to_all x2, waiting for transfers between devices, exchange(): lax.all_to_all(blocks, 'head', split_axis=0, concat_axis=0, tiled=True)  17 us
    ppermute x4, starting transfers between devices, shifted(): return lax.ppermute(rows, 'blk', route)  16.9 us
    ppermute x4, waiting for transfers between devices, shifted(): return lax.ppermute(rows, 'blk', route)  15.1 us
    all_to_all x2, starting transfers between devices, exchange(): lax.all_to_all(blocks, 'head', split_axis=0, concat_axis=0, tiled=True)  7.37 us
    pallas_call x1, Pallas kernels, per_device(): pl.pallas_call(attention, out_shape=(shape((window, 256), BF16), shape((w...  6.25 us
  transfers between devices with their start and end apart: 6, of which 4 were waited for; matrix products, arithmetic and copies ran while one was open for 0% of the time, Pallas kernels for 0%

profile of v1, /device:TPU:1, one launch (start us, length us, event | category | flops | bytes accessed | tf_op | source)
XLA Modules:
  0.0 101.7 jit_solution(10730014478038284681)
XLA Ops:
  0.6 2.0 %pack_first.1 = (bf16[32,16,768]{2,1,0:T(8,128)(2,1)}, bf16[16,2048]{1,0:T(8,128)(2,1)}) custom-call(bf16[16,8192]{1,0:T(8,128)(2,1)} %q_hbm.1, bf16[16,8192]{1,0:T(8,128)(2,1)} %g_hbm.1, bf16[16,1024]{1,0:T(8,128)(2,1)} %k_hbm.1, bf16[16,1024]{1,0:T(8,128)(2,1)} %v_hbm.1), custom_call_target="tpu_custom_call" | custom-call | tf_op jit(solution)/shard_map/pack_first/pallas_call | solution.py:240
  2.7 5.7 %collective-permute-start.1 = (bf16[16,2048]{1,0:T(8,128)(2,1)}, bf16[16,2048]{1,0:T(8,128)(2,1)S(1)}, u32[]{:S(2)}, u32[]{:S(2)}) collective-permute-start(bf16[16,2048]{1,0:T(8,128)(2,1)} %get-tuple-element.15), channel_id=1, source_target_pairs={{960,0},{992,32},{0,64},{32,96},{64,128},{96,160},{128,192},{160,2... | collective-permute-start | bytes 196616 | tf_op jit(solution)/shard_map/ppermute | solution.py:40
  8.4 3.5 %collective-permute-start = (bf16[16,2048]{1,0:T(8,128)(2,1)}, bf16[16,2048]{1,0:T(8,128)(2,1)S(1)}, u32[]{:S(2)}, u32[]{:S(2)}) collective-permute-start(bf16[16,2048]{1,0:T(8,128)(2,1)} %get-tuple-element.15), channel_id=1, source_target_pairs={{992,0},{0,32},{32,64},{64,96},{96,128},{128,160},{160,192},{192,2... | collective-permute-start | bytes 196616 | tf_op jit(solution)/shard_map/ppermute | solution.py:40
  11.9 12.3 %collective-permute-done.1.kv2_ref = bf16[16,2048]{1,0:T(8,128)(2,1)S(1)} collective-permute-done((bf16[16,2048]{1,0:T(8,128)(2,1)}, bf16[16,2048]{1,0:T(8,128)(2,1)S(1)}, u32[]{:S(2)}, u32[]{:S(2)}) %collective-permute-start.1) | collective-permute-done | bytes 65568 | tf_op jit(solution)/shard_map/ppermute | solution.py:40
  24.3 2.7 %collective-permute-done.kv1_ref = bf16[16,2048]{1,0:T(8,128)(2,1)S(1)} collective-permute-done((bf16[16,2048]{1,0:T(8,128)(2,1)}, bf16[16,2048]{1,0:T(8,128)(2,1)S(1)}, u32[]{:S(2)}, u32[]{:S(2)}) %collective-permute-start) | collective-permute-done | bytes 65568 | tf_op jit(solution)/shard_map/ppermute | solution.py:40
  27.0 0.1 pack_lags.1
  27.1 19.4 %all_to_all.20 = bf16[32,16,512]{2,1,0:T(8,128)(2,1)S(1)} all-to-all(bf16[32,16,512]{2,1,0:T(8,128)(2,1)S(1)} %pack_lags.1), channel_id=1, replica_groups=mesh['blk'=32,'head'=32] {'head'}, dimensions={0} | all-to-all | bytes 1048576 | tf_op jit(solution)/shard_map/all_to_all | solution.py:34
  46.5 3.7 %all-to-all-start = ((bf16[32,16,768]{2,1,0:T(8,128)(2,1)}), bf16[32,16,768]{2,1,0:T(8,128)(2,1)S(1)}, u32[]{:S(2)}, u32[]{:S(2)}) async-start(bf16[32,16,768]{2,1,0:T(8,128)(2,1)} %get-tuple-element.14), calls=%async_computation | async-start | bytes 1572864 | tf_op jit(solution)/shard_map/all_to_all | solution.py:34
  50.2 0.0 copy-start
  50.2 0.7 copy-done
  50.9 0.1 copy.10
  51.0 0.1 reshape.26.order_ref
  51.1 13.3 %all-to-all-done = bf16[32,16,768]{2,1,0:T(8,128)(2,1)S(1)} async-done(((bf16[32,16,768]{2,1,0:T(8,128)(2,1)}), bf16[32,16,768]{2,1,0:T(8,128)(2,1)S(1)}, u32[]{:S(2)}, u32[]{:S(2)}) %all-to-all-start) | async-done | bytes 786464 | tf_op jit(solution)/shard_map/all_to_all | solution.py:34
  64.3 6.3 %attention.1 = (bf16[512,256]{1,0:T(8,128)(2,1)}, bf16[512,512]{1,0:T(8,128)(2,1)S(1)}, bf16[512,512]{1,0:T(8,128)(2,1)}) custom-call(s32[64]{0:T(128)S(1)} %reshape.26.order_ref, s32[1]{0:T(128)} %bitcast.blk_ref, bf16[512,768]{1,0:T(8,128)(2,1)S(1)} %bitcast.5, bf16[512,512]{1,0:T(8,128)(2,1)S(1)} %bitcast.6), custom_call_target="tpu_custom_call" | custom-call | tf_op jit(solution)/shard_map/attention/pallas_call | solution.py:265
  70.6 15.2 %all_to_all.21.in_ref = bf16[32,16,512]{2,1,0:T(8,128)(2,1)S(1)} all-to-all(bf16[32,16,512]{2,1,0:T(8,128)(2,1)S(1)} %bitcast.7), channel_id=1, replica_groups=mesh['blk'=32,'head'=32] {'head'}, dimensions={0} | all-to-all | bytes 1048576 | tf_op jit(solution)/shard_map/all_to_all | solution.py:34
  85.8 3.7 %all-to-all-start.2 = ((bf16[32,16,512]{2,1,0:T(8,128)(2,1)}), bf16[32,16,512]{2,1,0:T(8,128)(2,1)S(1)}, u32[]{:S(2)}, u32[]{:S(2)}) async-start(bf16[32,16,512]{2,1,0:T(8,128)(2,1)} %bitcast.3), calls=%async_computation.2 | async-start | bytes 1048576 | tf_op jit(solution)/shard_map/all_to_all | solution.py:34
  89.5 0.1 unpack_lags.1
  89.5 3.4 %collective-permute-start.2 = (bf16[16,2048]{1,0:T(8,128)(2,1)S(1)}, bf16[16,2048]{1,0:T(8,128)(2,1)S(1)}, u32[]{:S(2)}, u32[]{:S(2)}) collective-permute-start(bf16[16,2048]{1,0:T(8,128)(2,1)S(1)} %get-tuple-element.19), channel_id=1, source_target_pairs={{32,0},{64,32},{96,64},{128,96},{160,128},{192,160},{224,192},{256... | collective-permute-start | bytes 196616 | tf_op jit(solution)/shard_map/ppermute | solution.py:40
  93.0 4.3 %collective-permute-start.3 = (bf16[16,2048]{1,0:T(8,128)(2,1)S(1)}, bf16[16,2048]{1,0:T(8,128)(2,1)S(1)}, u32[]{:S(2)}, u32[]{:S(2)}) collective-permute-start(bf16[16,2048]{1,0:T(8,128)(2,1)S(1)} %get-tuple-element.20), channel_id=1, source_target_pairs={{64,0},{96,32},{128,64},{160,96},{192,128},{224,160},{256,192},{28... | collective-permute-start | bytes 196616 | tf_op jit(solution)/shard_map/ppermute | solution.py:40
  97.2 3.8 %all-to-all-done.2.in_ref = bf16[32,16,512]{2,1,0:T(8,128)(2,1)S(1)} async-done(((bf16[32,16,512]{2,1,0:T(8,128)(2,1)}), bf16[32,16,512]{2,1,0:T(8,128)(2,1)S(1)}, u32[]{:S(2)}, u32[]{:S(2)}) %all-to-all-start.2) | async-done | bytes 524320 | tf_op jit(solution)/shard_map/all_to_all | solution.py:34
  101.0 0.0 collective-permute-done.2.one_ref
  101.0 0.0 collective-permute-done.3.two_ref
  101.0 0.7 unpack_last.1
Async XLA Ops:
  2.7 21.6 %collective-permute-start.1 = (bf16[16,2048]{1,0:T(8,128)(2,1)}, bf16[16,2048]{1,0:T(8,128)(2,1)S(1)}, u32[]{:S(2)}, u32[]{:S(2)}) collective-permute-start(bf16[16,2048]{1,0:T(8,128)(2,1)} %get-tuple-element.15), channel_id=1, source_target_pairs={{960,0},{992,32},{0,64},{32,96},{64,128},{96,160},{128,192},{160,2... | collective-permute-start | bytes 196616 | tf_op jit(solution)/shard_map/ppermute | solution.py:40
  8.4 18.6 %collective-permute-start = (bf16[16,2048]{1,0:T(8,128)(2,1)}, bf16[16,2048]{1,0:T(8,128)(2,1)S(1)}, u32[]{:S(2)}, u32[]{:S(2)}) collective-permute-start(bf16[16,2048]{1,0:T(8,128)(2,1)} %get-tuple-element.15), channel_id=1, source_target_pairs={{992,0},{0,32},{32,64},{64,96},{96,128},{128,160},{160,192},{192,2... | collective-permute-start | bytes 196616 | tf_op jit(solution)/shard_map/ppermute | solution.py:40
  46.5 17.9 %all-to-all-start = ((bf16[32,16,768]{2,1,0:T(8,128)(2,1)}), bf16[32,16,768]{2,1,0:T(8,128)(2,1)S(1)}, u32[]{:S(2)}, u32[]{:S(2)}) async-start(bf16[32,16,768]{2,1,0:T(8,128)(2,1)} %get-tuple-element.14), calls=%async_computation | async-start | bytes 1572864 | tf_op jit(solution)/shard_map/all_to_all | solution.py:34
  50.2 0.7 copy-start
  85.8 15.2 %all-to-all-start.2 = ((bf16[32,16,512]{2,1,0:T(8,128)(2,1)}), bf16[32,16,512]{2,1,0:T(8,128)(2,1)S(1)}, u32[]{:S(2)}, u32[]{:S(2)}) async-start(bf16[32,16,512]{2,1,0:T(8,128)(2,1)} %bitcast.3), calls=%async_computation.2 | async-start | bytes 1048576 | tf_op jit(solution)/shard_map/all_to_all | solution.py:34
  89.5 11.5 %collective-permute-start.2 = (bf16[16,2048]{1,0:T(8,128)(2,1)S(1)}, bf16[16,2048]{1,0:T(8,128)(2,1)S(1)}, u32[]{:S(2)}, u32[]{:S(2)}) collective-permute-start(bf16[16,2048]{1,0:T(8,128)(2,1)S(1)} %get-tuple-element.19), channel_id=1, source_target_pairs={{32,0},{64,32},{96,64},{128,96},{160,128},{192,160},{224,192},{256... | collective-permute-start | bytes 196616 | tf_op jit(solution)/shard_map/ppermute | solution.py:40
  93.0 8.0 %collective-permute-start.3 = (bf16[16,2048]{1,0:T(8,128)(2,1)S(1)}, bf16[16,2048]{1,0:T(8,128)(2,1)S(1)}, u32[]{:S(2)}, u32[]{:S(2)}) collective-permute-start(bf16[16,2048]{1,0:T(8,128)(2,1)S(1)} %get-tuple-element.20), channel_id=1, source_target_pairs={{64,0},{96,32},{128,64},{160,96},{192,128},{224,160},{256,192},{28... | collective-permute-start | bytes 196616 | tf_op jit(solution)/shard_map/ppermute | solution.py:40

commit v2 on v1

v2 whole, which is shorter than its diff:
```python
import math

import jax
import jax.numpy as jnp
from jax import lax
from jax.experimental import pallas as pl
from jax.experimental.pallas import tpu as pltpu
from jax.sharding import PartitionSpec as P


KEY_VALUE_HEADS = 8
HEAD_SIZE = 128
COPIES = 4
HALF = 256
NEG_BIG = -1e30
SCALE = 1.0 / math.sqrt(HEAD_SIZE)
SCALE_LOG2 = SCALE * math.log2(math.e)

F32 = jnp.float32
BF16 = jnp.bfloat16

VMEM = pl.BlockSpec(memory_space=pltpu.VMEM)
SMEM = pl.BlockSpec(memory_space=pltpu.SMEM)


PARAMS = pltpu.CompilerParams(vmem_limit_bytes=16 * 1024 * 1024)


def head_cols(head):
    return slice(head * HEAD_SIZE, (head + 1) * HEAD_SIZE)


def exchange(blocks):
    return lax.all_to_all(blocks, "head", split_axis=0, concat_axis=0, tiled=True)


def shifted(rows, distance):
    count = lax.axis_size("blk")
    route = [((i - distance) % count, i) for i in range(count)]
    return lax.ppermute(rows, "blk", route)


def join_rows(k_hbm, v_hbm, kv_ref, sems):
    moves = [
        pltpu.make_async_copy(k_hbm, kv_ref.at[:, 0:1024], sems.at[0]),
        pltpu.make_async_copy(v_hbm, kv_ref.at[:, 1024:2048], sems.at[1]),
    ]
    for move in moves:
        move.start()
    for move in moves:
        move.wait()


def pack_own(order_ref, blk_ref, kv_ref, q_ref, g_ref, out_ref, facts_ref):
    count = order_ref.shape[0]
    for lag in range(3):
        block = lax.rem(blk_ref[0] + (count - lag), count)
        first, second = order_ref[block, 0], order_ref[block, 1]
        facts_ref[2 * lag] = jnp.where(first < second, 0, HALF)
        facts_ref[2 * lag + 1] = jnp.minimum(first, second)
    for peer in range(out_ref.shape[0]):
        group = peer // COPIES
        cols = slice(2 * peer * HEAD_SIZE, 2 * (peer + 1) * HEAD_SIZE)
        out_ref[peer, :, 0:256] = q_ref[:, cols]
        out_ref[peer, :, 256:512] = g_ref[:, cols]
        out_ref[peer, :, 512:640] = kv_ref[:, head_cols(group)]
        out_ref[peer, :, 640:768] = kv_ref[:, head_cols(group + KEY_VALUE_HEADS)]


def pack_lags(own_ref, kv1_ref, kv2_ref, out_ref):
    for peer in range(out_ref.shape[0]):
        group = peer // COPIES
        out_ref[peer, :, 0:768] = own_ref[peer]
        for lag, kv_ref in enumerate((kv1_ref, kv2_ref), start=1):
            at = 512 + lag * 256
            out_ref[peer, :, at : at + 128] = kv_ref[:, head_cols(group)]
            out_ref[peer, :, at + 128 : at + 256] = kv_ref[:, head_cols(group + KEY_VALUE_HEADS)]


def sum_copies(in_ref, group, cols):
    total = in_ref[group * COPIES, :, cols].astype(F32)
    for copy in range(1, COPIES):
        total = total + in_ref[group * COPIES + copy, :, cols].astype(F32)
    return total


def unpack_lags(in_ref, one_ref, two_ref):
    for group in range(KEY_VALUE_HEADS):
        for lag, out_ref in enumerate((one_ref, two_ref), start=1):
            for part in range(2):
                at = 256 + lag * 256 + part * 128
                total = sum_copies(in_ref, group, slice(at, at + 128))
                out_ref[:, head_cols(group + part * KEY_VALUE_HEADS)] = total.astype(BF16)


def unpack_query(in_ref, gq_ref):
    for peer in range(in_ref.shape[0]):
        gq_ref[:, 2 * peer * HEAD_SIZE : 2 * (peer + 1) * HEAD_SIZE] = in_ref[peer, :, 0:256]


def unpack_last(in_ref, one_ref, two_ref, gk_ref, gv_ref):
    for group in range(KEY_VALUE_HEADS):
        for part, out_ref in enumerate((gk_ref, gv_ref)):
            at = 256 + part * 128
            total = sum_copies(in_ref, group, slice(at, at + 128))
            cols = head_cols(group + part * KEY_VALUE_HEADS)
            total = total + one_ref[:, cols].astype(F32) + two_ref[:, cols].astype(F32)
            out_ref[:, head_cols(group)] = total.astype(BF16)


def dot(a, b):
    return lax.dot_general(a, b, (((1,), (0,)), ((), ())), preferred_element_type=F32)


def dot_nt(a, b):
    return lax.dot_general(a, b, (((1,), (1,)), ((), ())), preferred_element_type=F32)


def attention(facts_ref, in_ref, attn_ref, out_ref, score_ref):
    low, chunk, low1, chunk1, low2, chunk2 = (facts_ref[i] for i in range(6))
    below1, below2 = chunk > chunk1, chunk > chunk2

    def at(offset):
        return pl.ds(pl.multiple_of(offset, HALF), HALF)

    lo, hi = at(low), at(HALF - low)
    lo1, hi1 = at(low1), at(HALF - low1)
    lo2, hi2 = at(low2), at(HALF - low2)
    q_dyn1, k_dyn1 = at(jnp.where(below1, low, HALF - low)), at(jnp.where(below1, low1, HALF - low1))
    q_dyn2, k_dyn2 = at(jnp.where(below2, low, HALF - low)), at(jnp.where(below2, low2, HALF - low2))

    tiles = (
        (lo, in_ref, lo, 512, "lo"),
        (hi, in_ref, hi, 512, "hi"),
        (hi, in_ref, lo, 512, "hi"),
        (hi, in_ref, lo1, 768, "hi"),
        (hi, in_ref, lo2, 1024, "hi"),
        (q_dyn1, in_ref, k_dyn1, 768, below1),
        (q_dyn2, in_ref, k_dyn2, 1024, below2),
    )
    diagonal = (0, 1)
    causal = lax.broadcasted_iota(jnp.int32, (HALF, HALF), 0) <= lax.broadcasted_iota(
        jnp.int32, (HALF, HALF), 1
    )

    def fold(side, new, low_value, high_value, op):
        if isinstance(side, str):
            if side == "lo":
                return op(low_value, new), high_value
            return low_value, (new if high_value is None else op(high_value, new))
        return (
            jnp.where(side, op(low_value, new), low_value),
            jnp.where(side, high_value, op(high_value, new)),
        )

    def pick(side, low_value, high_value):
        if isinstance(side, str):
            return low_value if side == "lo" else high_value
        return jnp.where(side, low_value, high_value)

    def first_or(op):
        return lambda old, new: new if old is None else op(old, new)

    add = first_or(jnp.add)
    larger = first_or(jnp.maximum)

    d_keys = [None] * len(tiles)
    d_values = [None] * len(tiles)
    keys_t, values_t = [], []
    for _, kv_ref, k_rows, col, _ in tiles:
        keys_t.append(kv_ref[k_rows, col : col + 128].T)
        values_t.append(kv_ref[k_rows, col + 128 : col + 256].T)

    for head in range(2):
        q_cols = head_cols(head)
        g_cols = slice(256 + head * HEAD_SIZE, 256 + (head + 1) * HEAD_SIZE)
        max_lo = max_hi = None
        for index, (q_rows, kv_ref, k_rows, col, side) in enumerate(tiles):
            score = dot_nt(kv_ref[k_rows, col : col + 128], in_ref[q_rows, q_cols]) * SCALE_LOG2
            if index in diagonal:
                score = jnp.where(causal, score, NEG_BIG)
            score_ref[index] = score
            max_lo, max_hi = fold(side, jnp.max(score, axis=0, keepdims=True), max_lo, max_hi, larger)
        sum_lo = sum_hi = None
        for index, (_, _, _, _, side) in enumerate(tiles):
            weights = jnp.exp2(score_ref[index] - pick(side, max_lo, max_hi))
            score_ref[index] = weights
            sum_lo, sum_hi = fold(side, jnp.sum(weights, axis=0, keepdims=True), sum_lo, sum_hi, add)
        inv_lo, inv_hi = 1.0 / sum_lo, 1.0 / sum_hi
        out_lo = out_hi = None
        for index, (_, _, _, _, side) in enumerate(tiles):
            probs = score_ref[index] * pick(side, inv_lo, inv_hi)
            score_ref[index] = probs
            part = dot(values_t[index], probs.astype(BF16))
            out_lo, out_hi = fold(side, part, out_lo, out_hi, add)
        attn_lo, attn_hi = out_lo.T.astype(BF16), out_hi.T.astype(BF16)
        attn_ref[lo, q_cols] = attn_lo
        attn_ref[hi, q_cols] = attn_hi
        delta_lo = jnp.sum(
            (attn_lo.astype(F32) * in_ref[lo, g_cols].astype(F32)).T, axis=0, keepdims=True
        )
        delta_hi = jnp.sum(
            (attn_hi.astype(F32) * in_ref[hi, g_cols].astype(F32)).T, axis=0, keepdims=True
        )
        dq_lo = dq_hi = None
        for index, (q_rows, kv_ref, k_rows, col, side) in enumerate(tiles):
            probs = score_ref[index]
            grads = in_ref[q_rows, g_cols]
            d_probs = dot_nt(kv_ref[k_rows, col + 128 : col + 256], grads)
            d_scores = (probs * (d_probs - pick(side, delta_lo, delta_hi))).astype(BF16)
            d_values[index] = add(d_values[index], dot(probs.astype(BF16), grads))
            d_keys[index] = add(d_keys[index], dot(d_scores, in_ref[q_rows, q_cols]))
            part = dot(keys_t[index], d_scores)
            dq_lo, dq_hi = fold(side, part, dq_lo, dq_hi, add)
        out_ref[lo, q_cols] = (dq_lo * SCALE).T.astype(BF16)
        out_ref[hi, q_cols] = (dq_hi * SCALE).T.astype(BF16)

    for part, scale, found in ((0, SCALE, d_keys), (1, 1.0, d_values)):
        cols = slice(256 + part * 128, 256 + (part + 1) * 128)
        out_ref[hi, cols] = (found[1] * scale).astype(BF16)
        out_ref[lo, cols] = ((found[0] + found[2]) * scale).astype(BF16)
        for lag, (below, lo_k, hi_k) in enumerate(((below1, lo1, hi1), (below2, lo2, hi2))):
            at_lag = 512 + lag * 256 + part * 128
            cols = slice(at_lag, at_lag + 128)
            always, extra = found[3 + lag], found[5 + lag]
            out_ref[lo_k, cols] = (jnp.where(below, always + extra, always) * scale).astype(BF16)
            out_ref[hi_k, cols] = (jnp.where(below, 0.0, extra) * scale).astype(BF16)


def per_device(query, key, value, grad_out, order):
    peers = lax.axis_size("head")
    rows = query.shape[0]
    window = peers * rows
    shape = jax.ShapeDtypeStruct

    hbm = pl.BlockSpec(memory_space=pltpu.HBM)
    kv = pl.pallas_call(
        join_rows,
        out_shape=shape((rows, 2048), BF16),
        in_specs=[hbm] * 2,
        out_specs=VMEM,
        scratch_shapes=[pltpu.SemaphoreType.DMA((2,))],
        name="join_rows",
    )(key, value)
    kv2, kv1 = shifted(kv, 2), shifted(kv, 1)
    blk = lax.axis_index("blk").astype(jnp.int32).reshape(1)
    own, facts = pl.pallas_call(
        pack_own,
        out_shape=(shape((peers, rows, 768), BF16), shape((8,), jnp.int32)),
        in_specs=[SMEM, SMEM, VMEM, VMEM, VMEM],
        out_specs=(VMEM, SMEM),
        compiler_params=PARAMS,
        name="pack_own",
    )(order, blk, kv, query, grad_out)
    packed = pl.pallas_call(
        pack_lags,
        out_shape=shape((peers, rows, 1280), BF16),
        in_specs=[VMEM] * 3,
        out_specs=VMEM,
        compiler_params=PARAMS,
        name="pack_lags",
    )(own, kv1, kv2)
    arrived = exchange(packed).reshape(window, 1280)

    attn, grads = pl.pallas_call(
        attention,
        out_shape=(shape((window, 256), BF16), shape((window, 1024), BF16)),
        in_specs=[SMEM, VMEM],
        out_specs=(VMEM, VMEM),
        scratch_shapes=[pltpu.VMEM((7, HALF, HALF), F32)],
        compiler_params=PARAMS,
        name="attention",
    )(facts, arrived)

    back = exchange(grads.reshape(peers, rows, 1024))
    one, two = pl.pallas_call(
        unpack_lags,
        out_shape=(shape((rows, 2048), BF16),) * 2,
        in_specs=[VMEM],
        out_specs=(VMEM, VMEM),
        compiler_params=PARAMS,
        name="unpack_lags",
    )(back)
    two, one = shifted(two, -2), shifted(one, -1)
    grad_query = pl.pallas_call(
        unpack_query,
        out_shape=shape((rows, 8192), BF16),
        in_specs=[VMEM],
        out_specs=VMEM,
        compiler_params=PARAMS,
        name="unpack_query",
    )(back)
    grad_key, grad_value = pl.pallas_call(
        unpack_last,
        out_shape=(shape((rows, 1024), BF16),) * 2,
        in_specs=[VMEM] * 3,
        out_specs=(VMEM,) * 2,
        compiler_params=PARAMS,
        name="unpack_last",
    )(back, one, two)
    return attn, grad_query, grad_key, grad_value


def solution(mesh):
    tokens = P(("blk", "head"), None)
    return jax.shard_map(
        per_device,
        mesh=mesh,
        in_specs=(tokens, tokens, tokens, tokens, P()),
        out_specs=(P("blk", "head"), tokens, tokens, tokens),
        check_vma=False,
    )
```

time: 102 us -> 93.1 us (0.913)
  waiting for transfers between devices: 32.1 us -> 12.5 us
  blocking collectives: 34.6 us -> 48.4 us
  starting transfers between devices: 24.3 us -> 17.2 us
  local copies, waits for them, and re-layouts: 0.86 us -> 3.5 us
  Pallas kernels: 9.16 us -> 10.3 us
    all_to_all x2 -> x0, waiting for transfers between devices: 17 us -> none  [exchange(): lax.all_to_all(blocks, 'head', split_axis=0, concat_axis=0, tiled=True)]
    all_to_all x2, blocking collectives: 34.6 us -> 48.4 us  [exchange(): lax.all_to_all(blocks, 'head', split_axis=0, concat_axis=0, tiled=True)]
    all_to_all x2 -> x0, starting transfers between devices: 7.37 us -> none  [exchange(): lax.all_to_all(blocks, 'head', split_axis=0, concat_axis=0, tiled=True)]
    unnamed x3 -> x7, local copies, waits for them, and re-layouts: 0.76 us -> 3.5 us
    ppermute x4, waiting for transfers between devices: 15.1 us -> 12.5 us  [shifted(): return lax.ppermute(rows, 'blk', route)]
    pallas_call x3 -> x5, Pallas kernels: 2.83 us -> 4.38 us  [the longest x1 1.43 us: per_device(): pl.pallas_call(pack_own, out_shape=(shape((peers, rows, 768), BF16), shap...]
  transfers between devices with their start and end apart: 6 -> 4, of which waited for: 4 -> 3; matrix products, arithmetic and copies ran while one was open for 0% -> 1% of each run, Pallas kernels for 0% -> 2%
where the time goes in v2:
time: 93.1 us; the launch traced here: 92.6 us
  blocking collectives  48.4 us (52%)
  starting transfers between devices  17.2 us (18%)
  waiting for transfers between devices  12.5 us (13%)
  Pallas kernels  10.3 us (11%)
  local copies, waits for them, and re-layouts  3.5 us (4%)
    all_to_all x2, blocking collectives, exchange(): lax.all_to_all(blocks, 'head', split_axis=0, concat_axis=0, tiled=True)  48.4 us
    ppermute x4, starting transfers between devices, shifted(): return lax.ppermute(rows, 'blk', route)  17.2 us
    ppermute x4, waiting for transfers between devices, shifted(): return lax.ppermute(rows, 'blk', route)  12.5 us
    pallas_call x1, Pallas kernels, per_device(): pl.pallas_call(attention, out_shape=(shape((window, 256), BF16), shape((w...  5.81 us
    unnamed x7, local copies, waits for them, and re-layouts  3.5 us
  transfers between devices with their start and end apart: 4, of which 3 were waited for; matrix products, arithmetic and copies ran while one was open for 1% of the time, Pallas kernels for 2%

profile of v2, /device:TPU:1, one launch (start us, length us, event | category | flops | bytes accessed | tf_op | source)
XLA Modules:
  0.0 92.6 jit_solution(16734982401099929901)
XLA Ops:
  0.6 1.4 %join_rows.1.kv_ref = bf16[16,2048]{1,0:T(8,128)(2,1)} custom-call(bf16[16,1024]{1,0:T(8,128)(2,1)} %k_hbm.1, bf16[16,1024]{1,0:T(8,128)(2,1)} %v_hbm.1), custom_call_target="tpu_custom_call" | custom-call | tf_op jit(solution)/shard_map/join_rows/pallas_call | solution.py:237
  2.1 5.7 %collective-permute-start.1 = (bf16[16,2048]{1,0:T(8,128)(2,1)}, bf16[16,2048]{1,0:T(8,128)(2,1)S(1)}, u32[]{:S(2)}, u32[]{:S(2)}) collective-permute-start(bf16[16,2048]{1,0:T(8,128)(2,1)} %join_rows.1.kv_ref), channel_id=1, source_target_pairs={{960,0},{992,32},{0,64},{32,96},{64,128},{96,160},{128,192},{160,2... | collective-permute-start | bytes 196616 | tf_op jit(solution)/shard_map/ppermute | solution.py:40
  7.8 3.5 %collective-permute-start = (bf16[16,2048]{1,0:T(8,128)(2,1)}, bf16[16,2048]{1,0:T(8,128)(2,1)S(1)}, u32[]{:S(2)}, u32[]{:S(2)}) collective-permute-start(bf16[16,2048]{1,0:T(8,128)(2,1)} %join_rows.1.kv_ref), channel_id=1, source_target_pairs={{992,0},{0,32},{32,64},{64,96},{96,128},{128,160},{160,192},{192,2... | collective-permute-start | bytes 196616 | tf_op jit(solution)/shard_map/ppermute | solution.py:40
  11.3 0.8 copy.9.order_ref
  12.1 0.0 copy-start
  12.1 0.9 %copy-done = bf16[16,8192]{1,0:T(8,128)(2,1)S(1)} copy-done((bf16[16,8192]{1,0:T(8,128)(2,1)S(1)}, bf16[16,8192]{1,0:T(8,128)(2,1)}, u32[]{:S(2)}) %copy-start) | copy-done | bytes 262168
  13.1 0.0 copy-start.1
  13.1 0.9 %copy-done.1 = bf16[16,8192]{1,0:T(8,128)(2,1)S(1)} copy-done((bf16[16,8192]{1,0:T(8,128)(2,1)S(1)}, bf16[16,8192]{1,0:T(8,128)(2,1)}, u32[]{:S(2)}) %copy-start.1) | copy-done | bytes 262168
  14.0 0.0 copy-start.2
  14.0 0.8 copy-done.2
  14.8 1.4 %pack_own.1 = (bf16[32,16,768]{2,1,0:T(8,128)(2,1)S(1)}, s32[8]{0:T(128)S(1)}) custom-call(s32[32,2]{1,0:T(8,128)S(1)} %copy.9.order_ref, s32[1]{0:T(128)} %bitcast.blk_ref, bf16[16,2048]{1,0:T(8,128)(2,1)S(1)} %copy-done.2, bf16[16,8192]{1,0:T(8,128)(2,1)S(1)} %copy-done, bf16[16,8192]{1,0:T(8,128)(2,1)S(1)} %copy-done.1), custom_call_target="tpu_custom_call" | custom-call | tf_op jit(solution)/shard_map/pack_own/pallas_call | solution.py:247
  16.3 7.4 %collective-permute-done.1.kv2_ref = bf16[16,2048]{1,0:T(8,128)(2,1)S(1)} collective-permute-done((bf16[16,2048]{1,0:T(8,128)(2,1)}, bf16[16,2048]{1,0:T(8,128)(2,1)S(1)}, u32[]{:S(2)}, u32[]{:S(2)}) %collective-permute-start.1) | collective-permute-done | bytes 65568 | tf_op jit(solution)/shard_map/ppermute | solution.py:40
  23.7 2.7 %collective-permute-done.kv1_ref = bf16[16,2048]{1,0:T(8,128)(2,1)S(1)} collective-permute-done((bf16[16,2048]{1,0:T(8,128)(2,1)}, bf16[16,2048]{1,0:T(8,128)(2,1)S(1)}, u32[]{:S(2)}, u32[]{:S(2)}) %collective-permute-start) | collective-permute-done | bytes 65568 | tf_op jit(solution)/shard_map/ppermute | solution.py:40
  26.4 0.1 pack_lags.1
  26.5 28.0 %all_to_all.10 = bf16[32,16,1280]{2,1,0:T(8,128)(2,1)S(1)} all-to-all(bf16[32,16,1280]{2,1,0:T(8,128)(2,1)S(1)} %pack_lags.1), channel_id=1, replica_groups=mesh['blk'=32,'head'=32] {'head'}, dimensions={0} | all-to-all | bytes 2621440 | tf_op jit(solution)/shard_map/all_to_all | solution.py:34
  54.5 5.8 %attention.1 = (bf16[512,256]{1,0:T(8,128)(2,1)}, bf16[512,1024]{1,0:T(8,128)(2,1)S(1)}) custom-call(s32[8]{0:T(128)S(1)} %get-tuple-element.12.facts_ref, bf16[512,1280]{1,0:T(8,128)(2,1)S(1)} %bitcast.3), custom_call_target="tpu_custom_call" | custom-call | tf_op jit(solution)/shard_map/attention/pallas_call | solution.py:265
  60.3 20.4 %all_to_all.11.in_ref = bf16[32,16,1024]{2,1,0:T(8,128)(2,1)S(1)} all-to-all(bf16[32,16,1024]{2,1,0:T(8,128)(2,1)S(1)} %bitcast.4), channel_id=1, replica_groups=mesh['blk'=32,'head'=32] {'head'}, dimensions={0} | all-to-all | bytes 2097152 | tf_op jit(solution)/shard_map/all_to_all | solution.py:34
  80.7 0.1 unpack_lags.1
  80.8 3.4 %collective-permute-start.2 = (bf16[16,2048]{1,0:T(8,128)(2,1)S(1)}, bf16[16,2048]{1,0:T(8,128)(2,1)S(1)}, u32[]{:S(2)}, u32[]{:S(2)}) collective-permute-start(bf16[16,2048]{1,0:T(8,128)(2,1)S(1)} %get-tuple-element.16), channel_id=1, source_target_pairs={{32,0},{64,32},{96,64},{128,96},{160,128},{192,160},{224,192},{256... | collective-permute-start | bytes 196616 | tf_op jit(solution)/shard_map/ppermute | solution.py:40
  84.2 4.5 %collective-permute-start.3 = (bf16[16,2048]{1,0:T(8,128)(2,1)S(1)}, bf16[16,2048]{1,0:T(8,128)(2,1)S(1)}, u32[]{:S(2)}, u32[]{:S(2)}) collective-permute-start(bf16[16,2048]{1,0:T(8,128)(2,1)S(1)} %get-tuple-element.17), channel_id=1, source_target_pairs={{64,0},{96,32},{128,64},{160,96},{192,128},{224,160},{256,192},{28... | collective-permute-start | bytes 196616 | tf_op jit(solution)/shard_map/ppermute | solution.py:40
  88.8 0.7 unpack_query.1
  89.5 0.0 collective-permute-done.2.one_ref
  89.5 2.4 %collective-permute-done.3.two_ref = bf16[16,2048]{1,0:T(8,128)(2,1)S(1)} collective-permute-done((bf16[16,2048]{1,0:T(8,128)(2,1)S(1)}, bf16[16,2048]{1,0:T(8,128)(2,1)S(1)}, u32[]{:S(2)}, u32[]{:S(2)}) %collective-permute-start.3) | collective-permute-done | bytes 65568 | tf_op jit(solution)/shard_map/ppermute | solution.py:40
  91.9 0.7 unpack_last.1
Async XLA Ops:
  2.1 21.6 %collective-permute-start.1 = (bf16[16,2048]{1,0:T(8,128)(2,1)}, bf16[16,2048]{1,0:T(8,128)(2,1)S(1)}, u32[]{:S(2)}, u32[]{:S(2)}) collective-permute-start(bf16[16,2048]{1,0:T(8,128)(2,1)} %join_rows.1.kv_ref), channel_id=1, source_target_pairs={{960,0},{992,32},{0,64},{32,96},{64,128},{96,160},{128,192},{160,2... | collective-permute-start | bytes 196616 | tf_op jit(solution)/shard_map/ppermute | solution.py:40
  7.8 18.6 %collective-permute-start = (bf16[16,2048]{1,0:T(8,128)(2,1)}, bf16[16,2048]{1,0:T(8,128)(2,1)S(1)}, u32[]{:S(2)}, u32[]{:S(2)}) collective-permute-start(bf16[16,2048]{1,0:T(8,128)(2,1)} %join_rows.1.kv_ref), channel_id=1, source_target_pairs={{992,0},{0,32},{32,64},{64,96},{96,128},{128,160},{160,192},{192,2... | collective-permute-start | bytes 196616 | tf_op jit(solution)/shard_map/ppermute | solution.py:40
  12.1 0.9 %copy-start = (bf16[16,8192]{1,0:T(8,128)(2,1)S(1)}, bf16[16,8192]{1,0:T(8,128)(2,1)}, u32[]{:S(2)}) copy-start(bf16[16,8192]{1,0:T(8,128)(2,1)} %q_ref.1) | copy-start | bytes 786436
  13.1 0.9 %copy-start.1 = (bf16[16,8192]{1,0:T(8,128)(2,1)S(1)}, bf16[16,8192]{1,0:T(8,128)(2,1)}, u32[]{:S(2)}) copy-start(bf16[16,8192]{1,0:T(8,128)(2,1)} %g_ref.1) | copy-start | bytes 786436
  14.0 0.8 copy-start.2
  80.8 8.7 %collective-permute-start.2 = (bf16[16,2048]{1,0:T(8,128)(2,1)S(1)}, bf16[16,2048]{1,0:T(8,128)(2,1)S(1)}, u32[]{:S(2)}, u32[]{:S(2)}) collective-permute-start(bf16[16,2048]{1,0:T(8,128)(2,1)S(1)} %get-tuple-element.16), channel_id=1, source_target_pairs={{32,0},{64,32},{96,64},{128,96},{160,128},{192,160},{224,192},{256... | collective-permute-start | bytes 196616 | tf_op jit(solution)/shard_map/ppermute | solution.py:40
  84.2 7.7 %collective-permute-start.3 = (bf16[16,2048]{1,0:T(8,128)(2,1)S(1)}, bf16[16,2048]{1,0:T(8,128)(2,1)S(1)}, u32[]{:S(2)}, u32[]{:S(2)}) collective-permute-start(bf16[16,2048]{1,0:T(8,128)(2,1)S(1)} %get-tuple-element.17), channel_id=1, source_target_pairs={{64,0},{96,32},{128,64},{160,96},{192,128},{224,160},{256,192},{28... | collective-permute-start | bytes 196616 | tf_op jit(solution)/shard_map/ppermute | solution.py:40
